TPU v7x, 512 devices: a whole 4x4x16 slice. The times are simulated.
512 devices in a mesh: branch: 8 (over z_lo), dp: 64 (over x, y, z_hi, core).
Axes of the slice: x: 4, y: 4, z: 16 (z_hi: 2, z_lo: 8; z = z_hi * 8 + z_lo), core: 2. Of those that a mesh axis runs over, the one named last changes fastest.
Arguments:
- tokens: bfloat16 [512, 4096], P('dp'), may hold values from -6 to 6
- routes: int32 [512, 2], P('dp'), may hold values from 0 to 7, all different within a row; in each aligned block of 8 rows (0 to 7, 8 to 15, ...) at most 4 rows name the same one
- route_weights: float32 [512, 2], P('dp'), may hold values from 0.2 to 1
- norm_gains: float32 [8, 4096], P('branch'), may hold values from 0.25 to 1.75
- keyval_weights: bfloat16 [8, 4096, 2048], P('branch', 'dp'), may hold values from -0.09375 to 0.09375
- expert_gate: bfloat16 [8, 4096, 8192], P('branch', None, 'dp'), may hold values from -0.09375 to 0.09375
- expert_up: bfloat16 [8, 4096, 8192], P('branch', None, 'dp'), may hold values from -0.09375 to 0.09375
- expert_down: bfloat16 [8, 8192, 4096], P('branch', None, 'dp'), may hold values from -0.0625 to 0.0625
Outputs:
- mixed: bfloat16 [512, 4096], P('dp')
- merged_keyval: bfloat16 [4096, 2048], P('dp', 'branch')
Inputs may be any that keep to these rules, and one draw needn't show every extreme that they name: `routes`: each token names 2 different experts. Among the 8 tokens of one dp index at most 4 name one expert, a bound that some block reaches.
All inputs are finite; a program needn't handle non-finite values.
Results may differ from a plain program's by a relative error of at most 0.013.
Values may be sent and summed in bfloat16 or wider, within the bound.
No kernel may reach another device: no remote copies, remote signals or barrier semaphores. Data moves between devices by JAX's collectives and lax.ppermute only.
A program may use at most 64 MiB of HBM per device.

v0:
```python
import jax
import jax.numpy as jnp
from jax import lax
from jax.sharding import PartitionSpec as P


def merge_keyval(keyval_weights, branches):
    summed = lax.psum_scatter(
        keyval_weights[0].astype(jnp.float32).astype(jnp.bfloat16),
        "branch",
        scatter_dimension=1,
        tiled=True,
    ).astype(jnp.float32)
    return (summed / branches).astype(jnp.bfloat16)


def normalize(block_rows, gain_avg):
    widened = block_rows.astype(jnp.float32)
    inv_rms = lax.rsqrt(jnp.mean(widened * widened, axis=1, keepdims=True) + 1e-05)
    return (widened * inv_rms * gain_avg[None, :]).astype(jnp.bfloat16)


def local(
    tokens, routes, route_weights, norm_gains, keyval_weights, expert_gate, expert_up, expert_down
):
    branches = lax.axis_size("branch")
    expert = lax.axis_index("branch")
    tok_count = tokens.shape[0]
    capacity = min(tok_count, 4 * tok_count // branches)
    merged_keyval = merge_keyval(keyval_weights, branches)
    gain_avg = lax.psum(norm_gains[0], "branch") / branches
    matched = routes == expert
    chosen = jnp.any(matched, axis=1)
    weight_share = jnp.sum(jnp.where(matched, route_weights, jnp.zeros_like(route_weights)), axis=1)
    slot_index = jnp.cumsum(chosen.astype(jnp.int32)) - 1
    picks = (
        (slot_index[None, :] == jnp.arange(capacity, dtype=jnp.int32)[:, None]) & chosen[None, :]
    ).astype(jnp.bfloat16)
    source_rows = normalize(tokens, gain_avg)
    packed = jnp.dot(picks, source_rows, preferred_element_type=jnp.float32).astype(jnp.bfloat16)
    block_rows = lax.all_gather(packed, "dp", axis=0, tiled=True)
    gate_part = jnp.dot(block_rows, expert_gate[0], preferred_element_type=jnp.float32)
    up_part = jnp.dot(block_rows, expert_up[0], preferred_element_type=jnp.float32)
    hidden = (jax.nn.silu(gate_part) * up_part).astype(jnp.bfloat16)
    down_rows = expert_down[0]
    result_cols = lax.dot_general(
        down_rows,
        lax.all_gather(hidden, "dp", axis=1, tiled=True),
        (((0,), (1,)), ((), ())),
        preferred_element_type=jnp.float32,
    ).astype(jnp.bfloat16)
    own_slots = lax.all_to_all(result_cols, "dp", split_axis=1, concat_axis=0, tiled=True)
    returned = (
        lax.dot_general(
            picks, own_slots, (((0,), (1,)), ((), ())), preferred_element_type=jnp.float32
        )
        * weight_share[:, None]
    )
    expert_total = lax.psum(returned, "branch")
    mixed = (tokens.astype(jnp.float32) + expert_total).astype(jnp.bfloat16)
    return (mixed, merged_keyval)


def solution(mesh):
    in_specs = (
        P("dp", None),
        P("dp", None),
        P("dp", None),
        P("branch", None),
        P("branch", "dp", None),
        P("branch", None, "dp"),
        P("branch", None, "dp"),
        P("branch", None, "dp"),
    )
    out_specs = (P("dp", None), P("dp", "branch"))
    return jax.shard_map(local, mesh=mesh, in_specs=in_specs, out_specs=out_specs, check_vma=False)
```

profile of v0, /device:TPU:2, one launch (start us, length us, event | category | flops | bytes accessed | tf_op | source)
XLA Modules:
  0.0 531.0 jit_solution(3716925837076763852)
XLA Ops:
  8.1 0.8 fusion.21
  8.8 0.2 reduce-window.8
  9.0 59.9 %psum.14 = f32[4096]{0:T(1024)S(1)} all-reduce(f32[4096]{0:T(1024)} %bitcast.33), channel_id=1, replica_groups=mesh['branch'=8,'dp'=64] {'branch'}, use_global_device_ids=true, to_apply=%region_3.4 | all-reduce | flops 4096 | bytes 32768 | tf_op jit(solution)/shard_map/psum | solution.py:31
  68.9 1.0 fusion.7
  69.9 1.7 fusion
  71.7 108.6 %all-gather.6.cloned.1.call-done = bf16[64,4,4096]{2,1,0:T(4,128)(2,1)} async-done(((bf16[1,4,4096]{2,1,0:T(4,128)(2,1)}), bf16[64,4,4096]{2,1,0:T(4,128)(2,1)}) %all-gather.6.cloned.1.call-update) | async-done | bytes 2097168 | tf_op jit(solution)/shard_map/all_gather | solution.py:41
  180.3 2.5 reshape.52
  182.9 0.7 fusion.5
  183.6 0.5 copy-done.4
  184.1 1.3 fusion.1
  185.5 134.4 %all-gather.4.cloned.1.call-done = bf16[256,8192]{1,0:T(8,128)(2,1)} async-done(((bf16[256,128]{1,0:T(8,128)(2,1)}), bf16[256,8192]{1,0:T(8,128)(2,1)}) %all-gather.4.cloned.1.call-update) | async-done | bytes 4194320 | tf_op jit(solution)/shard_map/all_gather | solution.py:48
  319.9 3.9 fusion.2
  323.8 0.1 copy.12
  323.9 0.7 reshape.53
  324.6 7.4 %all-to-all-start = ((bf16[64,2,128]{2,1,0:T(2,128)(2,1)}), bf16[64,2,128]{2,1,0:T(2,128)(2,1)S(1)}, u32[]{:S(2)}, u32[]{:S(2)}) async-start(bf16[64,2,128]{2,1,0:T(2,128)(2,1)} %reshape.53), calls=%async_computation | async-start | bytes 65536 | tf_op jit(solution)/shard_map/all_to_all | solution.py:52
  332.1 0.5 reduce-scatter.2.cloned.1.call-update
  332.7 15.1 %all-to-all-done = bf16[64,2,128]{2,1,0:T(2,128)(2,1)S(1)} async-done(((bf16[64,2,128]{2,1,0:T(2,128)(2,1)}), bf16[64,2,128]{2,1,0:T(2,128)(2,1)S(1)}, u32[]{:S(2)}, u32[]{:S(2)}) %all-to-all-start) | async-done | bytes 32800 | tf_op jit(solution)/shard_map/all_to_all | solution.py:52
  347.8 0.1 reshape.54
  348.0 0.1 all_to_all.17
  348.1 0.9 convolution_multiply_fusion
  349.0 55.0 %reduce-scatter.2.cloned.1.call-done = bf16[64,256]{1,0:T(8,128)(2,1)} async-done(((bf16[64,2048]{1,0:T(8,128)(2,1)}), bf16[64,256]{1,0:T(8,128)(2,1)}) %reduce-scatter.2.cloned.1.call-update) | async-done | bytes 32784 | tf_op jit(solution)/shard_map/reduce_scatter | solution.py:8
  404.0 1.4 multiply_convert_fusion
  405.3 116.7 %all-reduce.2.cloned.1.call-done = f32[8,4096]{1,0:T(8,128)} async-done(((f32[8,4096]{1,0:T(8,128)}), f32[8,4096]{1,0:T(8,128)}) %all-reduce.2.cloned.1.call-update) | async-done | bytes 131088 | tf_op jit(solution)/shard_map/psum | solution.py:59
  522.1 1.5 fusion.10
  (23 shorter events, 0.3 us)
Async XLA Ops:
  8.0 174.8 %copy-start = (bf16[1,4096,128]{2,1,0:T(8,128)(2,1)S(1)}, bf16[1,4096,128]{2,1,0:T(8,128)(2,1)}, u32[]{:S(2)}) copy-start(bf16[1,4096,128]{2,1,0:T(8,128)(2,1)} %param.13) | copy-start | bytes 3145732
  8.0 172.3 %all-gather.6.cloned.1.call-start = ((), (), s32[]{:S(2)}) async-start(), calls=%async_computation.5 | async-start | bytes 2129920 | tf_op jit(solution)/shard_map/all_gather | solution.py:41
  71.6 248.3 %all-gather.4.cloned.1.call-start = ((), (), s32[]{:S(2)}) async-start(), calls=%async_computation.2 | async-start | bytes 4259840 | tf_op jit(solution)/shard_map/all_gather | solution.py:48
  182.8 1.2 copy-start.4
  185.4 147.3 %copy-start.2 = (s32[8,2]{0,1:T(2,128)S(1)}, s32[8,2]{0,1:T(2,128)}, u32[]{:S(2)}) copy-start(s32[8,2]{0,1:T(2,128)} %param.9) | copy-start | bytes 196
  185.4 147.3 %copy-start.3 = (f32[8,2]{0,1:T(2,128)S(1)}, f32[8,2]{0,1:T(2,128)}, u32[]{:S(2)}) copy-start(f32[8,2]{0,1:T(2,128)} %param.10) | copy-start | bytes 196
  185.5 336.6 %copy-start.1 = (bf16[8,4096]{1,0:T(8,128)(2,1)S(1)}, bf16[8,4096]{1,0:T(8,128)(2,1)}, u32[]{:S(2)}) copy-start(bf16[8,4096]{1,0:T(8,128)(2,1)} %param.8) | copy-start | bytes 196612
  324.6 23.2 %all-to-all-start = ((bf16[64,2,128]{2,1,0:T(2,128)(2,1)}), bf16[64,2,128]{2,1,0:T(2,128)(2,1)S(1)}, u32[]{:S(2)}, u32[]{:S(2)}) async-start(bf16[64,2,128]{2,1,0:T(2,128)(2,1)} %reshape.53), calls=%async_computation | async-start | bytes 65536 | tf_op jit(solution)/shard_map/all_to_all | solution.py:52
  332.1 71.9 %reduce-scatter.2.cloned.1.call-start = ((), (), s32[]{:S(2)}) async-start(), calls=%async_computation.4 | async-start | bytes 294912 | tf_op jit(solution)/shard_map/reduce_scatter | solution.py:8
  332.6 189.4 %all-reduce.2.cloned.1.call-start = ((), (), s32[]{:S(2)}) async-start(), calls=%async_computation.3 | async-start | bytes 262144 | tf_op jit(solution)/shard_map/psum | solution.py:59
Sparse Core Ops, SparseCore 0:
  71.7 108.5 all-gather.5
  185.6 134.2 all-gather.3
Sparse Core Ops, SparseCore 1:
  335.3 68.6 reduce-scatter.1
  406.7 115.3 all-reduce.1
where the time goes:
time: 532 us; the launch traced here: 531 us
  waiting for transfers between devices  430 us (81%)
  blocking collectives  59.9 us (11%)
  between operations  15.6 us (3%)
  matrix products  8.44 us (2%)
  starting transfers between devices  7.61 us (1%)
    all_gather x1, waiting for transfers between devices, local(): lax.all_gather(hidden, 'dp', axis=1, tiled=True)  134 us
    psum x1, waiting for transfers between devices, local(): expert_total = lax.psum(returned, 'branch')  117 us
    all_gather x1, waiting for transfers between devices, local(): block_rows = lax.all_gather(packed, 'dp', axis=0, tiled=True)  109 us
    psum x1, blocking collectives, local(): gain_avg = lax.psum(norm_gains[0], 'branch') / branches  59.9 us
    reduce_scatter x1, waiting for transfers between devices, merge_keyval(): lax.psum_scatter(keyval_weights[0].astype(jnp.float32).astype(jnp.bfloat1...  55 us
    all_to_all x1, waiting for transfers between devices, local(): lax.all_to_all(result_cols, 'dp', split_axis=1, concat_axis=0, tiled=True)  15.1 us
  transfers between devices with their start and end apart: 5, of which 5 were waited for; matrix products, arithmetic and copies ran while one was open for 0% of the time, Pallas kernels for 0%

commit v1 on v0

--- a/solution.py
+++ b/solution.py
@@ -2,6 +2,11 @@
 import jax.numpy as jnp
 from jax import lax
 from jax.sharding import PartitionSpec as P
+from jax.lax import all_gather
+
+
+def test_the_corner(named_axis, message):
+    return all_gather(message, named_axis).sum(axis=0)
 
 
 def merge_keyval(keyval_weights, branches):
@@ -56,7 +61,7 @@
         )
         * weight_share[:, None]
     )
-    expert_total = lax.psum(returned, "branch")
+    expert_total = test_the_corner("branch", returned)
     mixed = (tokens.astype(jnp.float32) + expert_total).astype(jnp.bfloat16)
     return (mixed, merged_keyval)
 

time: 532 us -> 477 us (0.90)
  waiting for transfers between devices: 430 us -> 376 us
    psum x1 -> x0, waiting for transfers between devices: 117 us -> none  [local(): expert_total = lax.psum(returned, 'branch')]
    all_gather x0 -> x1, waiting for transfers between devices: none -> 61.9 us  [test_the_corner(): return all_gather(message, named_axis).sum(axis=0)]
  transfers between devices with their start and end apart: 5 -> 5, of which waited for: 5 -> 5; matrix products, arithmetic and copies ran while one was open for 0% -> 1% of each run, Pallas kernels for 0% -> 0%
where the time goes in v1:
time: 477 us
  waiting for transfers between devices  376 us (79%)
  blocking collectives  59.9 us (13%)
  between operations  15.6 us (3%)
  matrix products  8.44 us (2%)
  starting transfers between devices  7.61 us (2%)
  other arithmetic  5.31 us (1%)
    all_gather x1, waiting for transfers between devices, local(): lax.all_gather(hidden, 'dp', axis=1, tiled=True)  134 us
    all_gather x1, waiting for transfers between devices, local(): block_rows = lax.all_gather(packed, 'dp', axis=0, tiled=True)  109 us
    all_gather x1, waiting for transfers between devices, test_the_corner(): return all_gather(message, named_axis).sum(axis=0)  61.9 us
    psum x1, blocking collectives, local(): gain_avg = lax.psum(norm_gains[0], 'branch') / branches  59.9 us
    reduce_scatter x1, waiting for transfers between devices, merge_keyval(): lax.psum_scatter(keyval_weights[0].astype(jnp.float32).astype(jnp.bfloat1...  55 us
    all_to_all x1, waiting for transfers between devices, local(): lax.all_to_all(result_cols, 'dp', split_axis=1, concat_axis=0, tiled=True)  15.1 us
  transfers between devices with their start and end apart: 5, of which 5 were waited for; matrix products, arithmetic and copies ran while one was open for 1% of the time, Pallas kernels for 0%

profile of v1, /device:TPU:2, one launch (start us, length us, event | category | flops | bytes accessed | tf_op | source)
XLA Modules:
  0.0 476.6 jit_solution(3314857556598803051)
XLA Ops:
  8.1 0.8 fusion.21
  8.8 0.2 reduce-window.8
  9.0 59.9 %psum.7 = f32[4096]{0:T(1024)S(1)} all-reduce(f32[4096]{0:T(1024)} %bitcast.35), channel_id=1, replica_groups=mesh['branch'=8,'dp'=64] {'branch'}, use_global_device_ids=true, to_apply=%region_3.4 | all-reduce | flops 4096 | bytes 32768 | tf_op jit(solution)/shard_map/psum | solution.py:36
  68.9 1.0 fusion.7
  69.9 1.7 fusion
  71.7 108.6 %all-gather.10.cloned.1.call-done = bf16[64,4,4096]{2,1,0:T(4,128)(2,1)} async-done(((bf16[1,4,4096]{2,1,0:T(4,128)(2,1)}), bf16[64,4,4096]{2,1,0:T(4,128)(2,1)}) %all-gather.10.cloned.1.call-update) | async-done | bytes 2097168 | tf_op jit(solution)/shard_map/all_gather | solution.py:46
  180.3 2.5 reshape.53
  182.9 0.7 fusion.5
  183.6 0.5 copy-done.4
  184.1 1.3 fusion.1
  185.5 134.4 %all-gather.6.cloned.1.call-done = bf16[256,8192]{1,0:T(8,128)(2,1)} async-done(((bf16[256,128]{1,0:T(8,128)(2,1)}), bf16[256,8192]{1,0:T(8,128)(2,1)}) %all-gather.6.cloned.1.call-update) | async-done | bytes 4194320 | tf_op jit(solution)/shard_map/all_gather | solution.py:53
  319.9 3.9 fusion.2
  323.8 0.1 copy.12
  323.9 0.7 reshape.54
  324.6 7.4 %all-to-all-start = ((bf16[64,2,128]{2,1,0:T(2,128)(2,1)}), bf16[64,2,128]{2,1,0:T(2,128)(2,1)S(1)}, u32[]{:S(2)}, u32[]{:S(2)}) async-start(bf16[64,2,128]{2,1,0:T(2,128)(2,1)} %reshape.54), calls=%async_computation | async-start | bytes 65536 | tf_op jit(solution)/shard_map/all_to_all | solution.py:57
  332.1 0.5 reduce-scatter.2.cloned.1.call-update
  332.7 15.1 %all-to-all-done = bf16[64,2,128]{2,1,0:T(2,128)(2,1)S(1)} async-done(((bf16[64,2,128]{2,1,0:T(2,128)(2,1)}), bf16[64,2,128]{2,1,0:T(2,128)(2,1)S(1)}, u32[]{:S(2)}, u32[]{:S(2)}) %all-to-all-start) | async-done | bytes 32800 | tf_op jit(solution)/shard_map/all_to_all | solution.py:57
  348.0 0.1 all_to_all.17
  348.1 0.9 convolution_multiply_fusion
  349.0 55.0 %reduce-scatter.2.cloned.1.call-done = bf16[64,256]{1,0:T(8,128)(2,1)} async-done(((bf16[64,2048]{1,0:T(8,128)(2,1)}), bf16[64,256]{1,0:T(8,128)(2,1)}) %reduce-scatter.2.cloned.1.call-update) | async-done | bytes 32784 | tf_op jit(solution)/shard_map/reduce_scatter | solution.py:13
  404.0 1.4 multiply_convert_fusion
  405.3 61.9 %all-gather.8.cloned.1.call-done = f32[64,4096]{1,0:T(8,128)} async-done(((f32[8,4096]{1,0:T(8,128)}), f32[64,4096]{1,0:T(8,128)}) %all-gather.8.cloned.1.call-update) | async-done | bytes 1048592 | tf_op jit(solution)/shard_map/all_gather | solution.py:9
  467.3 1.3 bitcast_reduce_fusion
  468.6 0.6 fusion.10
  (24 shorter events, 0.4 us)
Async XLA Ops:
  8.0 174.8 %copy-start = (bf16[1,4096,128]{2,1,0:T(8,128)(2,1)S(1)}, bf16[1,4096,128]{2,1,0:T(8,128)(2,1)}, u32[]{:S(2)}) copy-start(bf16[1,4096,128]{2,1,0:T(8,128)(2,1)} %param.13) | copy-start | bytes 3145732
  8.0 172.3 %all-gather.10.cloned.1.call-start = ((), (), s32[]{:S(2)}) async-start(), calls=%async_computation.5 | async-start | bytes 2129920 | tf_op jit(solution)/shard_map/all_gather | solution.py:46
  71.6 248.3 %all-gather.6.cloned.1.call-start = ((), (), s32[]{:S(2)}) async-start(), calls=%async_computation.2 | async-start | bytes 4259840 | tf_op jit(solution)/shard_map/all_gather | solution.py:53
  182.8 1.2 copy-start.4
  185.4 147.3 %copy-start.2 = (s32[8,2]{0,1:T(2,128)S(1)}, s32[8,2]{0,1:T(2,128)}, u32[]{:S(2)}) copy-start(s32[8,2]{0,1:T(2,128)} %param.9) | copy-start | bytes 196
  185.4 147.3 %copy-start.3 = (f32[8,2]{0,1:T(2,128)S(1)}, f32[8,2]{0,1:T(2,128)}, u32[]{:S(2)}) copy-start(f32[8,2]{0,1:T(2,128)} %param.10) | copy-start | bytes 196
  323.8 144.8 %copy-start.1 = (bf16[8,4096]{1,0:T(8,128)(2,1)S(1)}, bf16[8,4096]{1,0:T(8,128)(2,1)}, u32[]{:S(2)}) copy-start(bf16[8,4096]{1,0:T(8,128)(2,1)} %param.8) | copy-start | bytes 196612
  324.6 23.2 %all-to-all-start = ((bf16[64,2,128]{2,1,0:T(2,128)(2,1)}), bf16[64,2,128]{2,1,0:T(2,128)(2,1)S(1)}, u32[]{:S(2)}, u32[]{:S(2)}) async-start(bf16[64,2,128]{2,1,0:T(2,128)(2,1)} %reshape.54), calls=%async_computation | async-start | bytes 65536 | tf_op jit(solution)/shard_map/all_to_all | solution.py:57
  332.1 71.9 %reduce-scatter.2.cloned.1.call-start = ((), (), s32[]{:S(2)}) async-start(), calls=%async_computation.3 | async-start | bytes 294912 | tf_op jit(solution)/shard_map/reduce_scatter | solution.py:13
  332.6 134.6 %all-gather.8.cloned.1.call-start = ((), (), s32[]{:S(2)}) async-start(), calls=%async_computation.4 | async-start | bytes 1179648 | tf_op jit(solution)/shard_map/all_gather | solution.py:9
Sparse Core Ops, SparseCore 0:
  71.7 108.5 all-gather.9
  185.6 134.2 all-gather.5
Sparse Core Ops, SparseCore 1:
  335.3 68.6 reduce-scatter.1
  405.9 61.3 all-gather.7
